TPU v7x, 256 devices: a whole 4x4x8 slice. The times are simulated.
256 devices in a mesh: grp: 32 (over x, y, core), tp: 8 (over z).
Axes of the slice: x: 4, y: 4, z: 8, core: 2. Of those that a mesh axis runs over, the one named last changes fastest.
Arguments:
- hidden_in: bfloat16 [512, 2048], P('grp'), may hold values from -6 to 6
- norm_gain: bfloat16 [2048], replicated, may hold values from 0.099609375 to 1.8984375
- w_query: bfloat16 [2048, 2048], P(None, 'tp'), may hold values from -0.125 to 0.125
- w_keyval: bfloat16 [2048, 512], P(None, 'tp'), may hold values from -0.125 to 0.125
- w_output: bfloat16 [2048, 2048], P('tp'), may hold values from -0.125 to 0.125
- prefix_cache: bfloat16 [64, 512, 512], P('grp', 'tp'), may hold values from -130 to 130
- private_cache: bfloat16 [512, 512, 512], P('grp', 'tp'), may hold values from -130 to 130
- node_parent: int32 [64], replicated, may hold values from 0 to 3, as said below
- node_length: int32 [64], replicated, may hold values from 1 to 512, as said below
- request_node: int32 [512], replicated, may hold values from 4 to 63, as said below
- private_length: int32 [512], P('grp'), may hold values from 0 to 512, as said below
Outputs:
- hidden_out: bfloat16 [512, 2048], P('grp', 'tp')
- new_keyval: bfloat16 [512, 512], P('grp', 'tp')
Inputs may be any that keep to these rules, and one draw needn't show every extreme that they name: `node_parent`: nodes 0 to 3 are the tenants' roots and are their own parents; every other node's parent is a root, and every root has a child. `request_node`: request r belongs to tenant r // 128; its node is a non-root node whose parent is that tenant's root. `node_length`: the longest node has exactly 512 used slots. `private_length`: some request has exactly 512 used slots.
All inputs are finite; a program needn't handle non-finite values.
Results may differ from a plain program's by a relative error of at most 0.023.
Values may be sent and summed in bfloat16 or wider, within the bound.
A program may use at most 128 MiB of HBM per device.

v0:
```python
import math
import jax
import jax.numpy as jnp
from jax import lax
from jax.sharding import PartitionSpec as P

HEADS = 32
KV_HEADS = 4
HEAD_DIM = 64
TENANTS = 4


def combined_all(x, axis, combine):
    everything = jax.tree.map(
        lambda part, kind: lax.all_gather(part.astype(kind), axis),
        x,
        (jnp.bfloat16, jnp.bfloat16, jnp.bfloat16),
    )

    def take(k):
        return jax.tree.map(lambda part, own: part[k].astype(own.dtype), everything, x)

    return lax.fori_loop(
        1, lax.axis_size(axis), lambda k, so_far: combine(so_far, take(k)), take(0)
    )


def rms_norm(values, scale_gain):
    floats = values.astype(jnp.float32)
    spread = jnp.mean(floats * floats, axis=-1, keepdims=True)
    return (floats * lax.rsqrt(spread + 1e-05) * scale_gain.astype(jnp.float32)).astype(
        jnp.bfloat16
    )


def rotate(head_rows, position):
    half_dim = head_rows.shape[-1] // 2
    freq_index = jnp.arange(half_dim, dtype=jnp.float32)
    frequency = jnp.exp(freq_index * (-2.0 * math.log(10000.0) / head_rows.shape[-1]))
    angles = position[:, None, None] * frequency[None, None, :]
    cosine = jnp.cos(angles)
    sine_part = jnp.sin(angles)
    front_half = head_rows[..., :half_dim]
    back_half = head_rows[..., half_dim:]
    return jnp.concatenate(
        [front_half * cosine - back_half * sine_part, back_half * cosine + front_half * sine_part],
        axis=-1,
    )


def softmax_part(queries, key_rows, value_rows, valid, shared):
    row_count = queries.shape[0]
    grouped = queries.reshape(row_count, KV_HEADS, HEADS // KV_HEADS, HEAD_DIM)
    if shared:
        scores = jnp.einsum("nkgd,lkd->nkgl", grouped, key_rows, preferred_element_type=jnp.float32)
    else:
        scores = jnp.einsum(
            "nkgd,nlkd->nkgl", grouped, key_rows, preferred_element_type=jnp.float32
        )
    scores = scores * HEAD_DIM ** (-0.5)
    usable = valid[:, None, None, :]
    scores = jnp.where(usable, scores, -jnp.inf)
    maxima = jnp.maximum(jnp.max(scores, axis=-1), -1e30)
    weights = jnp.where(usable, jnp.exp(scores - maxima[..., None]), 0.0)
    totals = jnp.sum(weights, axis=-1)
    rounded = weights.astype(jnp.bfloat16)
    if shared:
        weighted = jnp.einsum(
            "nkgl,lkd->nkgd", rounded, value_rows, preferred_element_type=jnp.float32
        )
    else:
        weighted = jnp.einsum(
            "nkgl,nlkd->nkgd", rounded, value_rows, preferred_element_type=jnp.float32
        )
    return (weighted, maxima, totals)


def merge_pair(left_part, right_part):
    left_sum, left_max, left_total = left_part
    right_sum, right_max, right_total = right_part
    upper = jnp.maximum(left_max, right_max)
    left_factor = jnp.exp(left_max - upper)
    right_factor = jnp.exp(right_max - upper)
    merged_sum = left_sum * left_factor[..., None] + right_sum * right_factor[..., None]
    return (merged_sum, upper, left_total * left_factor + right_total * right_factor)


def add_token(weighted, maxima, totals, token_score, token_value, form):
    upper = jnp.maximum(maxima, token_score)
    former = jnp.exp(maxima - upper)
    fresh = jnp.exp(token_score - upper)
    summed = weighted * former[..., None] + jnp.einsum(
        form, fresh.astype(jnp.bfloat16), token_value, preferred_element_type=jnp.float32
    )
    return summed / (totals * former + fresh)[..., None]


def on_device(
    hidden_in,
    norm_gain,
    w_query,
    w_keyval,
    w_output,
    prefix_cache,
    private_cache,
    node_parent,
    node_length,
    request_node,
    private_length,
):
    grp_index = lax.axis_index("grp")
    tp_index = lax.axis_index("tp")
    req_dev = hidden_in.shape[0]
    total_req = request_node.shape[0]
    per_tenant = total_req // TENANTS
    share_count = HEADS // KV_HEADS
    key_width = KV_HEADS * HEAD_DIM
    local_heads = w_query.shape[1] // HEAD_DIM
    local_kv = w_keyval.shape[1] // HEAD_DIM
    slice_width = local_heads * HEAD_DIM
    node_dev = prefix_cache.shape[0]
    local_len = prefix_cache.shape[1]
    priv_len = private_cache.shape[1]
    scale_factor = HEAD_DIM ** (-0.5)
    normed = rms_norm(hidden_in, norm_gain)
    query = jnp.dot(normed, w_query, preferred_element_type=jnp.float32)
    keyval = jnp.dot(normed, w_keyval, preferred_element_type=jnp.float32)
    own_mid = lax.dynamic_slice_in_dim(request_node, grp_index * req_dev, req_dev)
    own_root = node_parent[own_mid]
    position = (node_length[own_root] + node_length[own_mid] + private_length).astype(jnp.float32)
    query_rot = (
        rotate(query.reshape(req_dev, local_heads, HEAD_DIM), position)
        .reshape(req_dev, slice_width)
        .astype(jnp.bfloat16)
    )
    kv_rows = keyval.reshape(req_dev, local_kv, HEAD_DIM)
    is_key = tp_index * local_kv + jnp.arange(local_kv) < KV_HEADS
    new_keyval = (
        jnp.where(is_key[None, :, None], rotate(kv_rows, position), kv_rows)
        .reshape(req_dev, local_kv * HEAD_DIM)
        .astype(jnp.bfloat16)
    )
    query_all, keyval_all = (
        lax.all_gather(query_rot, "tp", axis=1, tiled=True),
        lax.all_gather(new_keyval, "tp", axis=1, tiled=True),
    )
    everyone = lax.all_gather(query_all, "grp", axis=0, tiled=True)
    private_valid = (tp_index * priv_len + jnp.arange(priv_len))[None, :] < private_length[:, None]
    private_keys = private_cache[:, :, :key_width].reshape(req_dev, priv_len, KV_HEADS, HEAD_DIM)
    private_values = private_cache[:, :, key_width:].reshape(req_dev, priv_len, KV_HEADS, HEAD_DIM)
    private_part = softmax_part(query_all, private_keys, private_values, private_valid, False)
    slot_positions = tp_index * local_len + jnp.arange(local_len)
    node_parts = []
    for node_slot in range(node_dev):
        node_id = grp_index * node_dev + node_slot
        is_root = node_id < TENANTS
        member = jnp.where(is_root, node_parent[request_node] == node_id, request_node == node_id)
        order_key = jnp.where(member, 0, total_req) + jnp.arange(total_req)
        picked = lax.top_k(-order_key, per_tenant)[1]
        filled = jnp.arange(per_tenant) < jnp.sum(member.astype(jnp.int32))
        chosen = jnp.take(everyone, picked, axis=0)
        node_rows = prefix_cache[node_slot]
        node_keys = node_rows[:, :key_width].reshape(local_len, KV_HEADS, HEAD_DIM)
        node_values = node_rows[:, key_width:].reshape(local_len, KV_HEADS, HEAD_DIM)
        node_valid = (slot_positions < node_length[node_id])[None, :]
        weighted, maxima, totals = softmax_part(chosen, node_keys, node_values, node_valid, True)
        level_slot = jnp.where(is_root, 0, 1)
        node_parts.append((picked, filled, level_slot, weighted, maxima, totals))
    sum_rows = jnp.zeros((total_req, 2, HEADS * HEAD_DIM), jnp.float32)
    max_rows = jnp.zeros((total_req, 2, HEADS), jnp.float32)
    total_rows = jnp.zeros((total_req, 2, HEADS), jnp.float32)
    for entry in node_parts:
        picked, filled, level_slot, weighted, maxima, totals = entry
        keep = filled[:, None]
        sum_rows = sum_rows.at[picked, level_slot].add(
            jnp.where(keep, weighted.reshape(per_tenant, HEADS * HEAD_DIM), 0.0)
        )
        max_rows = max_rows.at[picked, level_slot].add(
            jnp.where(keep, maxima.reshape(per_tenant, HEADS), 0.0)
        )
        total_rows = total_rows.at[picked, level_slot].add(
            jnp.where(keep, totals.reshape(per_tenant, HEADS), 0.0)
        )
    back_sum, back_max, back_total = (
        lax.psum_scatter(sum_rows, "grp", scatter_dimension=0, tiled=True),
        lax.psum_scatter(max_rows, "grp", scatter_dimension=0, tiled=True),
        lax.psum_scatter(total_rows, "grp", scatter_dimension=0, tiled=True),
    )
    stat_shape = (req_dev, 2, KV_HEADS, share_count)
    back_sum = back_sum.reshape(req_dev, 2, KV_HEADS, share_count, HEAD_DIM)
    back_max = back_max.reshape(stat_shape)
    back_total = back_total.reshape(stat_shape)
    root_part = (back_sum[:, 0], back_max[:, 0], back_total[:, 0])
    mid_part = (back_sum[:, 1], back_max[:, 1], back_total[:, 1])
    local_sum, local_max, local_total = merge_pair(merge_pair(root_part, mid_part), private_part)
    full_sum, full_max, full_total = combined_all(
        (local_sum, local_max, local_total), "tp", merge_pair
    )
    grouped = query_all.reshape(req_dev, KV_HEADS, share_count, HEAD_DIM)
    token_keys = keyval_all[:, :key_width].reshape(req_dev, KV_HEADS, HEAD_DIM)
    token_values = keyval_all[:, key_width:].reshape(req_dev, KV_HEADS, HEAD_DIM)
    token_score = (
        jnp.einsum("nkgd,nkd->nkg", grouped, token_keys, preferred_element_type=jnp.float32)
        * scale_factor
    )
    attention_all = (
        add_token(full_sum, full_max, full_total, token_score, token_values, "nkg,nkd->nkgd")
        .reshape(req_dev, HEADS * HEAD_DIM)
        .astype(jnp.bfloat16)
    )
    attention = lax.dynamic_slice_in_dim(attention_all, tp_index * slice_width, slice_width, 1)
    projected = jnp.dot(attention, w_output, preferred_element_type=jnp.float32)
    summed = lax.psum_scatter(
        projected.astype(jnp.bfloat16), "tp", scatter_dimension=1, tiled=True
    ).astype(jnp.float32)
    out_width = summed.shape[1]
    residual = lax.dynamic_slice_in_dim(hidden_in, tp_index * out_width, out_width, 1).astype(
        jnp.float32
    )
    hidden_out = (summed + residual).astype(jnp.bfloat16)
    return (hidden_out, new_keyval)


def solution(mesh):
    placed = (
        P("grp", None),
        P(),
        P(None, "tp"),
        P(None, "tp"),
        P("tp", None),
        P("grp", "tp", None),
        P("grp", "tp", None),
        P(),
        P(),
        P(),
        P("grp"),
    )
    return jax.shard_map(
        on_device,
        mesh=mesh,
        in_specs=placed,
        out_specs=(P("grp", "tp"), P("grp", "tp")),
        check_vma=False,
    )
```

profile of v0, /device:TPU:10, one launch (start us, length us, event | category | flops | bytes accessed | tf_op | source)
XLA Modules:
  0.0 476.1 jit_solution(16032584762213668495)
XLA Ops:
  7.3 0.8 compare_select_fusion.3
  8.1 1.3 gather_fusion
  9.4 1.3 gather_fusion.2
  10.7 1.3 gather_fusion.1
  12.1 0.7 convert_element_type.137
  12.8 1.0 fusion.32
  13.8 1.6 fusion.59
  15.4 0.7 add_convert_fusion.2
  16.5 30.2 %all_gather.23 = bf16[16,2048]{1,0:T(8,128)(2,1)} all-gather(bf16[16,256]{1,0:T(8,128)(2,1)S(1)} %convert_element_type.140), channel_id=1, replica_groups=mesh['grp'=32,'tp'=8] {'tp'}, dimensions={1}, use_global_device_ids=true | all-gather | bytes 73728 | tf_op jit(solution)/shard_map/all_gather | solution.py:144
  46.7 0.9 slice_bitcast_fusion.2
  48.1 1.6 fusion.90
  49.7 2.1 fusion.87
  51.8 2.1 fusion.88
  53.8 2.1 fusion.89
  55.9 41.3 %convert_reduce_fusion = (s32[]{:T(128)}, pred[512]{0:T(512)(128)(4,1)S(1)}, s32[512]{0:T(512)S(1)}) fusion(s32[512]{0:T(512)} %param.24, s32[]{:T(128)S(6)} %add.231, pred[]{:T(512)S(6)} %lt.150, s32[]{:T(128)} %bitcast.67, s32[]{:T(128)} %bitcast.66, s32[]{:T(128)} %bitcast.65, s32[]{:T(128)} %bitcast.64, s32[]{:T(128)} %bitcast.63, s32[]{:T(128)} %bitcast.62, ...), kind=kLoop, calls=%fused_computation.153 | loop fusion | flops 68607 | bytes 4873 | tf_op jit(solution)/shard_map/reduce_sum | solution.py:160
  97.2 1.3 convert_reduce_fusion.1
  98.6 3.8 top_k.17
  102.3 3.8 top_k.24
  106.1 1.3 fusion.86
  107.5 0.6 iota_compare_fusion.1
  108.1 0.6 iota_compare_fusion
  108.8 1.3 broadcast_compare_fusion.1
  110.2 4.3 gather_fusion.3
  114.5 2.0 broadcast_select_fusion.3
  116.4 2.0 copy.74
  118.5 1.3 fusion.91
  119.9 0.9 copy-done.2
  121.2 1.7 gather_fusion.4
  122.9 1.2 broadcast_select_fusion.2
  124.3 0.3 fusion.92
  125.0 0.3 copy-done.9
  125.6 1.6 fusion.18
  127.2 1.3 copy.77
  128.5 1.4 broadcast_select_fusion.1
  129.9 2.1 fusion.16
  132.0 1.6 copy.81
  133.5 1.1 broadcast_select_fusion
  134.8 6.8 %scatter_fusion.4 = f32[512,2,32]{2,1,0:T(2,128)S(1)} fusion(f32[512,2,32]{2,1,0:T(2,128)S(1)} %broadcast.255.clone.1, s32[128]{0:T(128)S(1)} %fusion.77, f32[128,32]{1,0:T(8,128)S(1)} %copy.94), kind=kCustom, calls=%fused_computation.9 | custom fusion | flops 4096 | bytes 50176 | tf_op jit(solution)/shard_map/scatter-add | solution.py:181
  141.7 6.6 %scatter_fusion.2 = f32[512,2,32]{2,1,0:T(2,128)S(1)} fusion(f32[512,2,32]{2,1,0:T(2,128)S(1)} %broadcast.255.clone, s32[128]{0:T(128)S(1)} %fusion.77, f32[128,32]{1,0:T(8,128)S(1)} %copy.83), kind=kCustom, calls=%fused_computation.7 | custom fusion | flops 4096 | bytes 50176 | tf_op jit(solution)/shard_map/scatter-add | solution.py:178
  148.3 6.6 %scatter_fusion.5 = f32[512,2,32]{2,1,0:T(2,128)S(1)} fusion(f32[512,2,32]{2,1,0:T(2,128)S(1)} %scatter_fusion.4, s32[128]{0:T(128)S(1)} %fusion.78, f32[128,32]{1,0:T(8,128)S(1)} %copy.95), kind=kCustom, calls=%fused_computation.10 | custom fusion | flops 4096 | bytes 50176 | tf_op jit(solution)/shard_map/scatter-add | solution.py:181
  154.9 6.6 %scatter_fusion.3 = f32[512,2,32]{2,1,0:T(2,128)S(1)} fusion(f32[512,2,32]{2,1,0:T(2,128)S(1)} %scatter_fusion.2, s32[128]{0:T(128)S(1)} %fusion.78, f32[128,32]{1,0:T(8,128)S(1)} %copy.84), kind=kCustom, calls=%fused_computation.8 | custom fusion | flops 4096 | bytes 50176 | tf_op jit(solution)/shard_map/scatter-add | solution.py:178
  161.5 7.5 %broadcast_in_dim.180 = f32[512,2,2048]{2,1,0:T(2,128)} broadcast(f32[]{:T(128)} %constant.85.clone.1), dimensions={} | broadcast | bytes 8388612 | tf_op jit(solution)/shard_map/broadcast_in_dim | solution.py:169
  169.0 21.2 %scatter_fusion = f32[512,2,2048]{2,1,0:T(2,128)} fusion(f32[512,2,2048]{2,1,0:T(2,128)} %broadcast_in_dim.180, s32[128]{0:T(128)S(1)} %fusion.77, f32[128,2048]{1,0:T(8,128)S(1)} %broadcast_select_fusion.1), kind=kCustom, calls=%fused_computation.5 | custom fusion | flops 262144 | bytes 3146752 | tf_op jit(solution)/shard_map/scatter-add | solution.py:175
  190.3 22.7 %scatter_fusion.1 = f32[512,2,2048]{2,1,0:T(2,128)} fusion(f32[512,2,2048]{2,1,0:T(2,128)} %scatter_fusion, s32[128]{0:T(128)S(1)} %fusion.78, f32[128,2048]{1,0:T(8,128)} %broadcast_select_fusion), kind=kCustom, calls=%fused_computation.6 | custom fusion | flops 262144 | bytes 3146752 | tf_op jit(solution)/shard_map/scatter-add | solution.py:175
  213.1 0.7 copy-done.6
  214.4 0.4 reshape.467
  214.9 0.7 fusion.93
  215.7 1.4 reshape.468
  217.1 1.2 fusion.57
  218.5 24.5 %all-gather.1 = bf16[8,64,16]{1,2,0:T(8,128)(2,1)S(1)} all-gather(bf16[1,64,16]{1,2,0:T(8,128)(2,1)S(1)} %bitcast.283), channel_id=1, replica_groups=mesh['grp'=32,'tp'=8] {'tp'}, dimensions={0}, use_global_device_ids=true | all-gather | bytes 18432 | tf_op jit(solution)/shard_map/all_gather | solution.py:145
  243.3 0.6 dynamic-slice
  244.7 99.7 %all-reduce.8.cloned.1.call-done = (f32[512,2,2048]{2,1,0:T(2,128)}, f32[512,2,32]{2,1,0:T(2,128)}, f32[512,2,32]{2,1,0:T(2,128)}) async-done(((f32[512,2,2048]{2,1,0:T(2,128)}, f32[512,2,32]{2,1,0:T(2,128)}, f32[512,2,32]{2,1,0:T(2,128)}), (f32[512,2,2048]{2,1,0:T(2,128)}, f32[512,2,32]{2,1,0:T(2,128)}, f32[512,2,32]{2,1,0:T(2,128)})) %all-reduce.8.cloned.1.call-update) | async-done | bytes 8650768
  344.4 0.7 constant_dynamic-slice_fusion.3
  345.4 0.3 fusion.30
  345.7 0.7 constant_dynamic-slice_fusion.2
  346.6 26.0 %all_gather.28 = bf16[8,16,4,8]{1,3,2,0:T(8,128)(2,1)S(1)} all-gather(bf16[1,16,4,8]{1,3,2,0:T(8,128)(2,1)S(1)} %fusion.49), channel_id=1, replica_groups=mesh['grp'=32,'tp'=8] {'tp'}, dimensions={0}, use_global_device_ids=true | all-gather | bytes 9216 | tf_op jit(solution)/shard_map/all_gather | solution.py:15
  372.9 1.0 constant_dynamic-slice_fusion.4
  374.4 1.7 fusion.9
  376.1 26.8 %all-gather = bf16[128,4,8,64]{3,2,1,0:T(8,128)(2,1)S(1)} all-gather(bf16[16,4,8,64]{3,2,1,0:T(8,128)(2,1)S(1)} %fusion.9), channel_id=2, replica_groups=mesh['grp'=32,'tp'=8] {'tp'}, dimensions={0}, use_global_device_ids=true | all-gather | bytes 589824 | tf_op jit(solution)/shard_map/all_gather | solution.py:15
  402.9 24.6 %all_gather.27 = bf16[8,16,4,8]{1,3,2,0:T(8,128)(2,1)S(1)} all-gather(bf16[1,16,4,8]{1,3,2,0:T(8,128)(2,1)S(1)} %fusion.56), channel_id=1, replica_groups=mesh['grp'=32,'tp'=8] {'tp'}, dimensions={0}, use_global_device_ids=true | all-gather | bytes 9216 | tf_op jit(solution)/shard_map/all_gather | solution.py:15
  427.5 3.9 while.19
  431.9 0.9 convolution_convert_fusion
  432.9 35.4 %reduce-scatter.2.cloned.1.call-done = bf16[16,256]{1,0:T(8,128)(2,1)} async-done(((bf16[16,2048]{1,0:T(8,128)(2,1)}), bf16[16,256]{1,0:T(8,128)(2,1)}) %reduce-scatter.2.cloned.1.call-update) | async-done | bytes 8208 | tf_op jit(solution)/shard_map/reduce_scatter | solution.py:213
  468.2 1.3 add_convert_fusion.1
  (159 shorter events, 9.6 us)
Async XLA Ops:
  7.2 424.8 %copy-start = (bf16[256,2048]{1,0:T(8,128)(2,1)S(1)}, bf16[256,2048]{1,0:T(8,128)(2,1)}, u32[]{:S(2)}) copy-start(bf16[256,2048]{1,0:T(8,128)(2,1)} %param.19) | copy-start | bytes 3145732
  7.2 103.0 %all-gather.4.cloned.1.call-start = ((), (), s32[]{:S(2)}) async-start(), calls=%async_computation.1 | async-start | bytes 2162688 | tf_op jit(solution)/shard_map/all_gather | solution.py:147
  7.2 102.9 %copy-start.18 = (f32[32]{0:T(128)}, f32[32]{0:T(128)S(1)}, u32[]{:S(2)}) copy-start(f32[32]{0:T(128)S(1)} %multiply_exponential_fusion) | copy-start | bytes 388
  13.7 1.6 copy-start.21
  16.1 94.1 %copy-start.13 = (f32[16]{0:T(128)}, f32[16]{0:T(128)S(1)}, u32[]{:S(2)}) copy-start(f32[16]{0:T(128)S(1)} %add_convert_fusion.2) | copy-start | bytes 196
  46.7 297.8 %all-reduce.8.cloned.1.call-start = ((), (), s32[]{:S(2)}) async-start(), calls=%async_computation.3 | async-start | bytes 18874368
  108.1 16.5 %copy-start.17 = (pred[128]{0:T(512)(128)(4,1)}, pred[128]{0:T(512)(128)(4,1)S(1)}, u32[]{:S(2)}) copy-start(pred[128]{0:T(512)(128)(4,1)S(1)} %iota_compare_fusion.1) | copy-start | bytes 388
  108.8 16.2 %copy-start.15 = (pred[128]{0:T(512)(128)(4,1)}, pred[128]{0:T(512)(128)(4,1)S(1)}, u32[]{:S(2)}) copy-start(pred[128]{0:T(512)(128)(4,1)S(1)} %iota_compare_fusion) | copy-start | bytes 388
  110.0 9.8 %copy-start.12 = (pred[64]{0:T(512)(128)(4,1)}, pred[64]{0:T(512)(128)(4,1)S(1)}, u32[]{:S(2)}) copy-start(pred[64]{0:T(512)(128)(4,1)S(1)} %get-tuple-element.351) | copy-start | bytes 196
  110.0 14.6 %copy-start.11 = (pred[64]{0:T(512)(128)(4,1)}, pred[64]{0:T(512)(128)(4,1)S(1)}, u32[]{:S(2)}) copy-start(pred[64]{0:T(512)(128)(4,1)S(1)} %get-tuple-element.350) | copy-start | bytes 196
  110.2 11.0 %copy-start.1 = (bf16[512,2048]{1,0:T(8,128)(2,1)S(1)}, bf16[512,2048]{1,0:T(8,128)(2,1)}, u32[]{:S(2)}) copy-start(bf16[512,2048]{1,0:T(8,128)(2,1)} %all-gather.4.cloned.1.call-done) | copy-start | bytes 6291460
  119.8 1.0 copy-start.2
  119.8 1.2 copy-start.8
  124.7 0.6 copy-start.9
  127.2 6.3 %copy-start.16 = (pred[128]{0:T(512)(128)(4,1)S(1)}, pred[128]{0:T(512)(128)(4,1)}, u32[]{:S(2)}) copy-start(pred[128]{0:T(512)(128)(4,1)} %copy-done.15) | copy-start | bytes 388
  154.9 35.3 %copy-start.3 = (f32[512,2,32]{2,1,0:T(2,128)}, f32[512,2,32]{2,1,0:T(2,128)S(1)}, u32[]{:S(2)}) copy-start(f32[512,2,32]{2,1,0:T(2,128)S(1)} %scatter_fusion.5) | copy-start | bytes 393220
  161.5 28.7 %copy-start.4 = (f32[512,2,32]{2,1,0:T(2,128)}, f32[512,2,32]{2,1,0:T(2,128)S(1)}, u32[]{:S(2)}) copy-start(f32[512,2,32]{2,1,0:T(2,128)S(1)} %scatter_fusion.3) | copy-start | bytes 393220
  213.0 0.8 copy-start.6
  213.0 1.3 copy-start.5
  213.0 1.8 copy-start.20
  213.0 4.2 copy-start.7
  213.0 4.2 copy-start.22
  213.0 5.3 %copy-start.14 = (f32[16]{0:T(128)S(1)}, f32[16]{0:T(128)}, u32[]{:S(2)}) copy-start(f32[16]{0:T(128)} %copy-done.13) | copy-start | bytes 196
  213.0 5.3 %copy-start.19 = (f32[32]{0:T(128)S(1)}, f32[32]{0:T(128)}, u32[]{:S(2)}) copy-start(f32[32]{0:T(128)} %copy-done.18) | copy-start | bytes 388
  213.0 30.3 %copy-start.23 = (u32[256]{0:T(256)S(1)}, u32[256]{0:T(256)}, u32[]{:S(2)}) copy-start(u32[256]{0:T(256)} %constant.274) | copy-start | bytes 3076
  213.1 255.2 %reduce-scatter.2.cloned.1.call-start = ((), (), s32[]{:S(2)}) async-start(), calls=%async_computation.2 | async-start | bytes 73728 | tf_op jit(solution)/shard_map/reduce_scatter | solution.py:213
  218.5 214.3 %copy-start.10 = (bf16[16,64]{1,0:T(8,128)(2,1)}, bf16[16,64]{1,0:T(8,128)(2,1)S(1)}, u32[]{:S(2)}) copy-start(bf16[16,64]{1,0:T(8,128)(2,1)S(1)} %fusion.71) | copy-start | bytes 6148
Sparse Core Ops, SparseCore 0:
  46.8 46.4 all-gather.3
  213.2 131.2 all-reduce.7
  433.0 35.2 reduce-scatter.1
where the time goes:
time: 478 us; the launch traced here: 476 us
  other arithmetic  137 us (29%)
  waiting for transfers between devices  135 us (28%)
  blocking collectives  132 us (28%)
  local copies, waits for them, and re-layouts  44.5 us (9%)
  between operations  15.1 us (3%)
  matrix products  11.6 us (2%)
    unnamed x4, waiting for transfers between devices  99.7 us
    all_gather x3, blocking collectives, combined_all(): lax.all_gather(part.astype(kind), axis)  77.3 us
    scatter-add x2, other arithmetic, on_device(): sum_rows.at[picked, level_slot]  43.9 us
    reduce_sum x2, other arithmetic, on_device(): filled = jnp.arange(per_tenant) < jnp.sum(member.astype(jnp.int32))  42.6 us
    reduce_scatter x1, waiting for transfers between devices, on_device(): lax.psum_scatter(projected.astype(jnp.bfloat16), 'tp', scatter_dimension=...  35.4 us
    all_gather x1, blocking collectives, on_device(): lax.all_gather(query_rot, 'tp', axis=1, tiled=True)  30.2 us
    all_gather x1, blocking collectives, on_device(): lax.all_gather(new_keyval, 'tp', axis=1, tiled=True)  24.5 us
    scatter-add x2, other arithmetic, on_device(): total_rows.at[picked, level_slot]  13.4 us
  transfers between devices with their start and end apart: 3, of which 2 were waited for; matrix products, arithmetic and copies ran while one was open for 14% of the time, Pallas kernels for 0%

commit v1 on v0

--- a/solution.py
+++ b/solution.py
@@ -141,7 +141,9 @@
         .astype(jnp.bfloat16)
     )
     query_all, keyval_all = (
-        lax.all_gather(query_rot, "tp", axis=1, tiled=True),
+        jnp.concatenate(
+            lax.all_to_all(jnp.stack([query_rot] * lax.axis_size("tp")), "tp", 0, 0), axis=1
+        ),
         lax.all_gather(new_keyval, "tp", axis=1, tiled=True),
     )
     everyone = lax.all_gather(query_all, "grp", axis=0, tiled=True)

time: 478 us -> 464 us (0.971)
  blocking collectives: 132 us -> 118 us
    all_gather x1 -> x0, blocking collectives: 30.2 us -> none  [on_device(): lax.all_gather(query_rot, 'tp', axis=1, tiled=True)]
    all_to_all x0 -> x1, blocking collectives: none -> 16.6 us  [on_device(): lax.all_to_all(jnp.stack([query_rot] * lax.axis_size('tp')), 'tp', 0, 0)]
  transfers between devices with their start and end apart: 3 -> 3, of which waited for: 2 -> 2; matrix products, arithmetic and copies ran while one was open for 14% -> 15% of each run, Pallas kernels for 0% -> 0%
where the time goes in v1:
time: 464 us; the launch traced here: 462 us
  other arithmetic  138 us (30%)
  waiting for transfers between devices  132 us (28%)
  blocking collectives  118 us (25%)
  local copies, waits for them, and re-layouts  45.8 us (10%)
  between operations  15.1 us (3%)
  matrix products  11.5 us (2%)
    unnamed x4, waiting for transfers between devices  96.7 us
    all_gather x3, blocking collectives, combined_all(): lax.all_gather(part.astype(kind), axis)  77.3 us
    scatter-add x2, other arithmetic, on_device(): sum_rows.at[picked, level_slot]  43.9 us
    reduce_sum x2, other arithmetic, on_device(): filled = jnp.arange(per_tenant) < jnp.sum(member.astype(jnp.int32))  42.8 us
    reduce_scatter x1, waiting for transfers between devices, on_device(): lax.psum_scatter(projected.astype(jnp.bfloat16), 'tp', scatter_dimension=...  35.4 us
    all_gather x1, blocking collectives, on_device(): lax.all_gather(new_keyval, 'tp', axis=1, tiled=True)  24.5 us
    all_to_all x1, blocking collectives, on_device(): lax.all_to_all(jnp.stack([query_rot] * lax.axis_size('tp')), 'tp', 0, 0)  16.6 us
    scatter-add x2, other arithmetic, on_device(): total_rows.at[picked, level_slot]  13.4 us
  transfers between devices with their start and end apart: 3, of which 2 were waited for; matrix products, arithmetic and copies ran while one was open for 15% of the time, Pallas kernels for 0%

profile of v1, /device:TPU:10, one launch (start us, length us, event | category | flops | bytes accessed | tf_op | source)
XLA Modules:
  0.0 461.5 jit_solution(16765370477193713853)
XLA Ops:
  7.3 0.8 compare_select_fusion.3
  8.1 1.3 gather_fusion
  9.4 1.3 gather_fusion.2
  10.7 1.3 gather_fusion.1
  12.1 0.7 convert_element_type.139
  12.8 1.0 fusion.32
  13.8 1.6 fusion.59
  15.4 0.7 add_convert_fusion.2
  16.5 16.6 %all_to_all.5 = bf16[8,16,256]{2,1,0:T(8,128)(2,1)S(1)} all-to-all(bf16[8,16,256]{2,1,0:T(8,128)(2,1)S(1)} %stack.2), channel_id=1, replica_groups=mesh['grp'=32,'tp'=8] {'tp'}, dimensions={0} | all-to-all | bytes 131072 | tf_op jit(solution)/shard_map/all_to_all | solution.py:145
  33.1 0.6 copy.119
  33.8 0.9 slice_bitcast_fusion.2
  35.0 0.7 copy.79
  35.8 1.6 fusion.90
  37.4 2.1 fusion.87
  39.5 2.1 fusion.88
  41.5 2.1 fusion.89
  43.6 41.5 %convert_reduce_fusion = (s32[]{:T(128)}, pred[512]{0:T(512)(128)(4,1)S(1)}, s32[512]{0:T(512)S(1)}) fusion(s32[512]{0:T(512)} %param.24, s32[]{:T(128)S(6)} %add.231, pred[]{:T(512)S(6)} %lt.150, s32[]{:T(128)} %bitcast.67, s32[]{:T(128)} %bitcast.66, s32[]{:T(128)} %bitcast.65, s32[]{:T(128)} %bitcast.64, s32[]{:T(128)} %bitcast.63, s32[]{:T(128)} %bitcast.62, ...), kind=kLoop, calls=%fused_computation.153 | loop fusion | flops 68607 | bytes 4873 | tf_op jit(solution)/shard_map/reduce_sum | solution.py:162
  85.1 1.3 convert_reduce_fusion.1
  86.5 3.8 top_k.17
  90.3 3.8 top_k.24
  94.0 1.3 fusion.86
  95.3 0.6 iota_compare_fusion.1
  96.0 0.6 iota_compare_fusion
  96.7 1.2 broadcast_compare_fusion.1
  98.0 4.3 gather_fusion.3
  102.3 2.0 broadcast_select_fusion.3
  104.2 2.0 copy.77
  106.3 1.3 fusion.91
  107.7 0.9 copy-done.2
  109.0 1.7 gather_fusion.4
  110.7 1.2 broadcast_select_fusion.2
  112.1 0.3 fusion.92
  113.4 1.6 fusion.18
  115.0 1.3 copy.80
  116.3 1.4 broadcast_select_fusion.1
  117.7 2.1 fusion.16
  119.7 1.6 copy.84
  121.3 1.8 broadcast_select_fusion
  123.2 6.8 %scatter_fusion.4 = f32[512,2,32]{2,1,0:T(2,128)S(1)} fusion(f32[512,2,32]{2,1,0:T(2,128)S(1)} %broadcast.256.clone.1, s32[128]{0:T(128)S(1)} %fusion.77, f32[128,32]{1,0:T(8,128)S(1)} %copy.98), kind=kCustom, calls=%fused_computation.9 | custom fusion | flops 4096 | bytes 50176 | tf_op jit(solution)/shard_map/scatter-add | solution.py:183
  130.2 6.6 %scatter_fusion.2 = f32[512,2,32]{2,1,0:T(2,128)S(1)} fusion(f32[512,2,32]{2,1,0:T(2,128)S(1)} %broadcast.256.clone, s32[128]{0:T(128)S(1)} %fusion.77, f32[128,32]{1,0:T(8,128)S(1)} %copy.86), kind=kCustom, calls=%fused_computation.7 | custom fusion | flops 4096 | bytes 50176 | tf_op jit(solution)/shard_map/scatter-add | solution.py:180
  136.8 6.6 %scatter_fusion.5 = f32[512,2,32]{2,1,0:T(2,128)S(1)} fusion(f32[512,2,32]{2,1,0:T(2,128)S(1)} %scatter_fusion.4, s32[128]{0:T(128)S(1)} %fusion.78, f32[128,32]{1,0:T(8,128)S(1)} %copy.99), kind=kCustom, calls=%fused_computation.10 | custom fusion | flops 4096 | bytes 50176 | tf_op jit(solution)/shard_map/scatter-add | solution.py:183
  143.4 6.6 %scatter_fusion.3 = f32[512,2,32]{2,1,0:T(2,128)S(1)} fusion(f32[512,2,32]{2,1,0:T(2,128)S(1)} %scatter_fusion.2, s32[128]{0:T(128)S(1)} %fusion.78, f32[128,32]{1,0:T(8,128)S(1)} %copy.87), kind=kCustom, calls=%fused_computation.8 | custom fusion | flops 4096 | bytes 50176 | tf_op jit(solution)/shard_map/scatter-add | solution.py:180
  150.0 7.5 %broadcast_in_dim.180 = f32[512,2,2048]{2,1,0:T(2,128)} broadcast(f32[]{:T(128)} %constant.85.clone.1), dimensions={} | broadcast | bytes 8388612 | tf_op jit(solution)/shard_map/broadcast_in_dim | solution.py:171
  157.5 21.2 %scatter_fusion = f32[512,2,2048]{2,1,0:T(2,128)} fusion(f32[512,2,2048]{2,1,0:T(2,128)} %broadcast_in_dim.180, s32[128]{0:T(128)S(1)} %fusion.77, f32[128,2048]{1,0:T(8,128)S(1)} %broadcast_select_fusion.1), kind=kCustom, calls=%fused_computation.5 | custom fusion | flops 262144 | bytes 3146752 | tf_op jit(solution)/shard_map/scatter-add | solution.py:177
  178.7 22.7 %scatter_fusion.1 = f32[512,2,2048]{2,1,0:T(2,128)} fusion(f32[512,2,2048]{2,1,0:T(2,128)} %scatter_fusion, s32[128]{0:T(128)S(1)} %fusion.78, f32[128,2048]{1,0:T(8,128)} %broadcast_select_fusion), kind=kCustom, calls=%fused_computation.6 | custom fusion | flops 262144 | bytes 3146752 | tf_op jit(solution)/shard_map/scatter-add | solution.py:177
  201.5 1.1 copy-done.5
  202.8 0.4 reshape.473
  203.2 1.4 reshape.474
  204.6 1.2 fusion.57
  206.0 24.5 %all-gather.1 = bf16[8,64,16]{1,2,0:T(8,128)(2,1)S(1)} all-gather(bf16[1,64,16]{1,2,0:T(8,128)(2,1)S(1)} %bitcast.289), channel_id=1, replica_groups=mesh['grp'=32,'tp'=8] {'tp'}, dimensions={0}, use_global_device_ids=true | all-gather | bytes 18432 | tf_op jit(solution)/shard_map/all_gather | solution.py:147
  230.8 0.6 dynamic-slice
  232.2 0.8 fusion.93
  233.3 96.6 %all-reduce.8.cloned.1.call-done = (f32[512,2,2048]{2,1,0:T(2,128)}, f32[512,2,32]{2,1,0:T(2,128)}, f32[512,2,32]{2,1,0:T(2,128)}) async-done(((f32[512,2,2048]{2,1,0:T(2,128)}, f32[512,2,32]{2,1,0:T(2,128)}, f32[512,2,32]{2,1,0:T(2,128)}), (f32[512,2,2048]{2,1,0:T(2,128)}, f32[512,2,32]{2,1,0:T(2,128)}, f32[512,2,32]{2,1,0:T(2,128)})) %all-reduce.8.cloned.1.call-update) | async-done | bytes 8650768
  329.9 0.7 constant_dynamic-slice_fusion.3
  331.2 0.7 constant_dynamic-slice_fusion.2
  332.0 26.0 %all_gather.24 = bf16[8,16,4,8]{1,3,2,0:T(8,128)(2,1)S(1)} all-gather(bf16[1,16,4,8]{1,3,2,0:T(8,128)(2,1)S(1)} %fusion.49), channel_id=1, replica_groups=mesh['grp'=32,'tp'=8] {'tp'}, dimensions={0}, use_global_device_ids=true | all-gather | bytes 9216 | tf_op jit(solution)/shard_map/all_gather | solution.py:15
  358.4 1.0 constant_dynamic-slice_fusion.4
  359.8 1.7 fusion.9
  361.5 26.8 %all-gather = bf16[128,4,8,64]{3,2,1,0:T(8,128)(2,1)S(1)} all-gather(bf16[16,4,8,64]{3,2,1,0:T(8,128)(2,1)S(1)} %fusion.9), channel_id=2, replica_groups=mesh['grp'=32,'tp'=8] {'tp'}, dimensions={0}, use_global_device_ids=true | all-gather | bytes 589824 | tf_op jit(solution)/shard_map/all_gather | solution.py:15
  388.3 24.6 %all_gather.23 = bf16[8,16,4,8]{1,3,2,0:T(8,128)(2,1)S(1)} all-gather(bf16[1,16,4,8]{1,3,2,0:T(8,128)(2,1)S(1)} %fusion.56), channel_id=1, replica_groups=mesh['grp'=32,'tp'=8] {'tp'}, dimensions={0}, use_global_device_ids=true | all-gather | bytes 9216 | tf_op jit(solution)/shard_map/all_gather | solution.py:15
  413.0 3.9 while.19
  417.4 0.9 convolution_convert_fusion
  418.3 35.4 %reduce-scatter.2.cloned.1.call-done = bf16[16,256]{1,0:T(8,128)(2,1)} async-done(((bf16[16,2048]{1,0:T(8,128)(2,1)}), bf16[16,256]{1,0:T(8,128)(2,1)}) %reduce-scatter.2.cloned.1.call-update) | async-done | bytes 8208 | tf_op jit(solution)/shard_map/reduce_scatter | solution.py:215
  453.7 1.3 add_convert_fusion.1
  (158 shorter events, 9.8 us)
Async XLA Ops:
  7.2 410.3 %copy-start = (bf16[256,2048]{1,0:T(8,128)(2,1)S(1)}, bf16[256,2048]{1,0:T(8,128)(2,1)}, u32[]{:S(2)}) copy-start(bf16[256,2048]{1,0:T(8,128)(2,1)} %param.19) | copy-start | bytes 3145732
  7.2 90.8 %all-gather.4.cloned.1.call-start = ((), (), s32[]{:S(2)}) async-start(), calls=%async_computation.2 | async-start | bytes 2162688 | tf_op jit(solution)/shard_map/all_gather | solution.py:149
  7.2 27.5 %copy-start.16 = (f32[32]{0:T(128)}, f32[32]{0:T(128)S(1)}, u32[]{:S(2)}) copy-start(f32[32]{0:T(128)S(1)} %multiply_exponential_fusion) | copy-start | bytes 388
  13.7 1.6 copy-start.19
  16.1 18.7 %copy-start.12 = (f32[16]{0:T(128)}, f32[16]{0:T(128)S(1)}, u32[]{:S(2)}) copy-start(f32[16]{0:T(128)S(1)} %add_convert_fusion.2) | copy-start | bytes 196
  33.8 296.1 %all-reduce.8.cloned.1.call-start = ((), (), s32[]{:S(2)}) async-start(), calls=%async_computation.4 | async-start | bytes 18874368
  96.0 16.5 %copy-start.15 = (pred[128]{0:T(512)(128)(4,1)}, pred[128]{0:T(512)(128)(4,1)S(1)}, u32[]{:S(2)}) copy-start(pred[128]{0:T(512)(128)(4,1)S(1)} %iota_compare_fusion.1) | copy-start | bytes 388
  96.6 16.1 %copy-start.14 = (pred[128]{0:T(512)(128)(4,1)}, pred[128]{0:T(512)(128)(4,1)S(1)}, u32[]{:S(2)}) copy-start(pred[128]{0:T(512)(128)(4,1)S(1)} %iota_compare_fusion) | copy-start | bytes 388
  97.9 9.8 %copy-start.11 = (pred[64]{0:T(512)(128)(4,1)}, pred[64]{0:T(512)(128)(4,1)S(1)}, u32[]{:S(2)}) copy-start(pred[64]{0:T(512)(128)(4,1)S(1)} %get-tuple-element.351) | copy-start | bytes 196
  97.9 14.6 %copy-start.10 = (pred[64]{0:T(512)(128)(4,1)}, pred[64]{0:T(512)(128)(4,1)S(1)}, u32[]{:S(2)}) copy-start(pred[64]{0:T(512)(128)(4,1)S(1)} %get-tuple-element.350) | copy-start | bytes 196
  98.0 11.0 %copy-start.1 = (bf16[512,2048]{1,0:T(8,128)(2,1)S(1)}, bf16[512,2048]{1,0:T(8,128)(2,1)}, u32[]{:S(2)}) copy-start(bf16[512,2048]{1,0:T(8,128)(2,1)} %all-gather.4.cloned.1.call-done) | copy-start | bytes 6291460
  107.6 1.0 copy-start.2
  107.6 1.2 copy-start.7
  112.5 0.6 copy-start.8
  143.4 35.3 %copy-start.3 = (f32[512,2,32]{2,1,0:T(2,128)}, f32[512,2,32]{2,1,0:T(2,128)S(1)}, u32[]{:S(2)}) copy-start(f32[512,2,32]{2,1,0:T(2,128)S(1)} %scatter_fusion.5) | copy-start | bytes 393220
  150.0 28.7 %copy-start.4 = (f32[512,2,32]{2,1,0:T(2,128)}, f32[512,2,32]{2,1,0:T(2,128)S(1)}, u32[]{:S(2)}) copy-start(f32[512,2,32]{2,1,0:T(2,128)S(1)} %scatter_fusion.3) | copy-start | bytes 393220
  201.4 1.2 copy-start.5
  201.4 3.2 copy-start.6
  201.4 3.2 copy-start.20
  201.4 4.4 copy-start.13
  201.4 4.4 copy-start.17
  201.4 29.3 %copy-start.21 = (u32[256]{0:T(256)S(1)}, u32[256]{0:T(256)}, u32[]{:S(2)}) copy-start(u32[256]{0:T(256)} %constant.274) | copy-start | bytes 3076
  201.4 30.6 %copy-start.18 = (s32[16]{0:T(128)S(1)}, s32[16]{0:T(128)}, u32[]{:S(2)}) copy-start(s32[16]{0:T(128)} %param.25) | copy-start | bytes 196
  201.5 252.2 %reduce-scatter.2.cloned.1.call-start = ((), (), s32[]{:S(2)}) async-start(), calls=%async_computation.3 | async-start | bytes 73728 | tf_op jit(solution)/shard_map/reduce_scatter | solution.py:215
  206.0 207.0 %copy-start.9 = (bf16[16,64]{1,0:T(8,128)(2,1)}, bf16[16,64]{1,0:T(8,128)(2,1)S(1)}, u32[]{:S(2)}) copy-start(bf16[16,64]{1,0:T(8,128)(2,1)S(1)} %fusion.71) | copy-start | bytes 6148
Sparse Core Ops, SparseCore 0:
  33.9 43.4 all-gather.3
  201.6 128.2 all-reduce.7
  418.5 35.2 reduce-scatter.1
